TPU v7x, 32 devices: a whole 2x2x4 slice. The times are simulated.
32 devices in a mesh: plane: 4 (over y, x), tile: 8 (over z, core).
Axes of the slice: x: 2, y: 2, z: 4, core: 2. Of those that a mesh axis runs over, the one named last changes fastest.
Arguments:
- recording: bfloat16 [4, 8, 3, 4, 256, 128], P('plane', 'tile'), may hold values from -8 to 8
- start_vectors: float32 [4, 16, 32, 128], P('plane', 'tile'), may hold values from -5 to 5
- footprints: bfloat16 [4, 1024, 256], P('plane', 'tile'), may hold values from 0.00019931793 to 0.029907227
- source_row: int32 [4, 1024, 1], P('plane', 'tile'), may hold values from 0 to 5; in each aligned block of 128 rows (0 to 127, 128 to 255, ..., all dimensions but the last counted through in order) at most 32 rows name the same one
- footprint_block: int32 [4, 1024], P('plane', 'tile'), may hold values from 0 to 3
Outputs:
- temporal_factors: float32 [4, 16, 32, 128], P('plane', 'tile')
- traces: float32 [4, 1024, 128], P('plane', 'tile')
Inputs may be any that keep to these rules, and one draw needn't show every extreme that they name: `source_row`: among the 128 sources of one device at most 32 share a value, and some value is shared by exactly 32 of them.
All inputs are finite; a program needn't handle non-finite values.
Results may differ from a plain program's by a relative error of at most 0.0069.
Values may be sent and summed in bfloat16 or wider, within the bound.
No kernel may reach another device: no remote copies, remote signals or barrier semaphores. Data moves between devices by JAX's collectives and lax.ppermute only.
A program may use at most 64 MiB of HBM per device.

v0:
```python
import jax
import jax.numpy as jnp
from jax import lax
from jax.sharding import PartitionSpec as P

ITERS = 3


def from_behind(block, axis, distance):
    devices = range(lax.axis_size(axis))
    route = [(i - distance, i) for i in devices if i - distance in devices]
    return lax.ppermute(block, axis, route)


def compress_patches(patches, start_block):
    temporal = start_block
    spatial = None
    for step_index in range(ITERS):
        projection = jnp.einsum(
            "prf,pkf->prk",
            temporal.astype(jnp.bfloat16),
            patches,
            preferred_element_type=jnp.float32,
        )
        gram_matrix = jnp.einsum(
            "prk,psk->prs", projection, projection, precision=lax.Precision.HIGHEST
        )
        cholesky_factor = jnp.linalg.cholesky(gram_matrix)
        spatial = jax.scipy.linalg.solve_triangular(cholesky_factor, projection, lower=True).astype(
            jnp.bfloat16
        )
        temporal = jnp.einsum("prk,pkf->prf", spatial, patches, preferred_element_type=jnp.float32)
    return (spatial, temporal)


def on_device(recording, start_vectors, footprints, source_row, footprint_block):
    tile_count = lax.axis_size("tile")
    own_strip = recording[0, 0]
    cell_count = own_strip.shape[0]
    patch_count = cell_count - 1
    block_pixels = own_strip.shape[2]
    frame_count = own_strip.shape[3]
    pixel_total = lax.axis_size("plane") * tile_count * cell_count * 4 * block_pixels
    frame_sum = jnp.sum(own_strip, axis=(0, 1, 2), dtype=jnp.float32)
    background = lax.psum(frame_sum, ("plane", "tile")) / pixel_total
    centered = (own_strip.astype(jnp.float32) - background).astype(jnp.bfloat16)
    lower_strip = from_behind(centered, "tile", -2)
    stacked = jnp.stack([centered, lower_strip])
    patches = jnp.stack(
        [
            stacked[:, column_index : column_index + 2].reshape(16 * block_pixels, frame_count)
            for column_index in range(patch_count)
        ]
    )
    spatial, temporal = compress_patches(patches, start_vectors[0])
    rank_width = spatial.shape[1]
    temporal_rounded = temporal.astype(jnp.bfloat16)
    source_rows = source_row[0, :, 0]
    block_value = footprint_block[0]
    footprint_rows = footprints[0]
    source_count = source_rows.shape[0]
    row_span = tile_count - 2
    capacity = max(2, (3 * source_count + 2 * row_span - 1) // (2 * row_span))
    row_match = (source_rows[:, None] == jnp.arange(tile_count)[None, :]).astype(jnp.int32)
    position = jnp.sum(jnp.cumsum(row_match, axis=0) * row_match, axis=1) - 1
    slot_upper = source_rows * capacity + position
    slot_lower = (source_rows + 2) * capacity + position
    footprint_send = jnp.zeros((tile_count * capacity, 2, block_pixels), jnp.bfloat16)
    footprint_send = (
        footprint_send.at[slot_upper, 0].set(footprint_rows).at[slot_lower, 1].set(footprint_rows)
    )
    block_send = jnp.full((tile_count * capacity, 2), -1, jnp.int32)
    block_send = block_send.at[slot_upper, 0].set(block_value).at[slot_lower, 1].set(block_value)
    footprint_send = footprint_send.reshape(tile_count, capacity, 2, block_pixels)
    block_send = block_send.reshape(tile_count, capacity, 2)
    spatial_blocks = spatial.reshape(patch_count, rank_width, 16, block_pixels)
    patch_axis = jnp.arange(patch_count)[None, None, :, None]
    block_axis = jnp.arange(8)[None, None, None, :]
    footprint_in = lax.all_to_all(footprint_send, "tile", split_axis=0, concat_axis=0, tiled=True)
    codes_in = lax.all_to_all(block_send, "tile", split_axis=0, concat_axis=0, tiled=True)
    role_terms = []
    for half_index in range(2):
        strip_offset = 1 - half_index
        block_range = spatial_blocks[:, :, strip_offset * 8 : strip_offset * 8 + 8]
        projected = jnp.einsum(
            "nkb,prgb->nkpgr",
            footprint_in[:, :, half_index],
            block_range,
            preferred_element_type=jnp.float32,
        )
        block_codes = codes_in[:, :, half_index]
        column_cell = (block_codes // 4 + 1)[:, :, None, None]
        quarter = (block_codes % 4)[:, :, None, None]
        filled = (block_codes >= 0)[:, :, None, None]
        from_left = (patch_axis == column_cell - 1) & (block_axis == quarter + 4)
        from_right = (patch_axis == column_cell) & (block_axis == quarter)
        selector = ((from_left | from_right) & filled).astype(jnp.float32)
        coefficient = jnp.sum(selector[..., None] * projected, axis=3)
        role_terms.append(
            coefficient.reshape(
                coefficient.shape[0], coefficient.shape[1], patch_count * rank_width
            )
        )
    coefficient = jnp.stack(role_terms, 2).astype(jnp.bfloat16)
    replies = lax.all_to_all(coefficient, "tile", split_axis=0, concat_axis=0, tiled=True)
    reply_rows = replies.reshape(tile_count * capacity, 2, patch_count * rank_width)
    upper_coefs = reply_rows[slot_upper, 0].reshape(source_count, patch_count, rank_width)
    lower_coefs = reply_rows[slot_lower, 1].reshape(source_count, patch_count, rank_width)
    coef_table = jnp.concatenate(
        [upper_coefs, lower_coefs, jnp.zeros((source_count, 1, rank_width), jnp.bfloat16)], 1
    )
    shard_rows = lax.all_gather(temporal_rounded, "tile", axis=0, tiled=True)
    patch_number = shard_rows.shape[0]
    patch_index = jnp.arange(patch_number)
    owner_row = patch_index // patch_count
    patch_column = patch_index % patch_count
    lookup = jnp.where(
        owner_row[None, :] == source_rows[:, None],
        patch_column[None, :],
        jnp.where(
            owner_row[None, :] == source_rows[:, None] + 2,
            patch_count + patch_column[None, :],
            2 * patch_count,
        ),
    )
    weights = jnp.take_along_axis(coef_table, lookup[:, :, None], axis=1)
    weights = weights.reshape(source_count, patch_number * rank_width)
    summed = jnp.dot(
        weights,
        shard_rows.reshape(patch_number * rank_width, frame_count),
        preferred_element_type=jnp.float32,
    )
    traces = 0.25 * summed
    return (temporal[None], traces[None])


def solution(mesh):
    placed = (
        P("plane", "tile", None, None, None, None),
        P("plane", "tile", None, None),
        P("plane", "tile", None),
        P("plane", "tile", None),
        P("plane", "tile"),
    )
    return jax.shard_map(
        on_device,
        mesh=mesh,
        in_specs=placed,
        out_specs=(P("plane", "tile", None, None), P("plane", "tile", None)),
        check_vma=False,
    )
```

profile of v0, /device:TPU:0, one launch (start us, length us, event | category | flops | bytes accessed | tf_op | source)
XLA Modules:
  0.0 174.9 jit_solution(6968167123436777132)
XLA Ops:
  0.6 1.6 convert_reduce_fusion
  2.3 42.0 %psum.7 = f32[128]{0:T(128)S(1)} all-reduce(f32[128]{0:T(128)S(1)} %convert_reduce_fusion), channel_id=1, replica_groups=mesh['plane'=4,'tile'=8] {'plane','tile'}, use_global_device_ids=true, to_apply=%region_1.0 | all-reduce | flops 128 | bytes 1024 | tf_op jit(solution)/shard_map/psum | solution.py:45
  44.5 1.3 collective-permute-start
  46.3 6.8 %scatter_fusion = s32[256,2]{0,1:T(2,128)S(1)} fusion(s32[256,2]{0,1:T(2,128)S(1)} %broadcast_in_dim.81, s32[128]{0:T(128)S(1)} %get-tuple-element.28, s32[128]{0:T(128)S(1)} %bitcast.186), kind=kCustom, calls=%fused_computation.3 | custom fusion | bytes 2560 | tf_op jit(solution)/shard_map/scatter | solution.py:73
  53.2 6.8 %scatter_fusion.1 = s32[256,2]{0,1:T(2,128)S(1)} fusion(s32[256,2]{0,1:T(2,128)S(1)} %scatter_fusion, s32[128]{0:T(128)S(1)} %get-tuple-element.29, s32[128]{0:T(128)S(1)} %bitcast.187), kind=kCustom, calls=%fused_computation.4 | custom fusion | bytes 2560 | tf_op jit(solution)/shard_map/scatter | solution.py:73
  60.7 5.7 %all-to-all-start = ((s32[8,32,2]{1,2,0:T(2,128)}), s32[8,32,2]{1,2,0:T(2,128)S(1)}, u32[]{:S(2)}, u32[]{:S(2)}) async-start(s32[8,32,2]{1,2,0:T(2,128)} %copy.50), calls=%async_computation | async-start | bytes 16384 | tf_op jit(solution)/shard_map/all_to_all | solution.py:80
  67.1 6.8 %scatter_fusion.2 = bf16[256,2,256]{2,1,0:T(2,128)(2,1)S(1)} fusion(bf16[256,2,256]{2,1,0:T(2,128)(2,1)S(1)} %broadcast_in_dim.82, s32[128]{0:T(128)S(1)} %get-tuple-element.28, bf16[128,256]{1,0:T(8,128)(2,1)S(1)} %bitcast.172), kind=kCustom, calls=%fused_computation.5 | custom fusion | bytes 197632 | tf_op jit(solution)/shard_map/scatter | solution.py:70
  73.9 6.8 %scatter_fusion.3 = bf16[256,2,256]{2,1,0:T(2,128)(2,1)S(1)} fusion(bf16[256,2,256]{2,1,0:T(2,128)(2,1)S(1)} %scatter_fusion.2, s32[128]{0:T(128)S(1)} %get-tuple-element.29, bf16[128,256]{1,0:T(8,128)(2,1)S(1)} %bitcast.173), kind=kCustom, calls=%fused_computation.6 | custom fusion | bytes 197632 | tf_op jit(solution)/shard_map/scatter | solution.py:70
  81.6 5.1 %all-to-all-start.1 = ((bf16[8,32,2,256]{3,1,2,0:T(8,128)(2,1)}), bf16[8,32,2,256]{3,1,2,0:T(8,128)(2,1)}, u32[]{:S(2)}, u32[]{:S(2)}) async-start(bf16[8,32,2,256]{3,1,2,0:T(8,128)(2,1)} %copy.52), calls=%async_computation.1 | async-start | bytes 524288 | tf_op jit(solution)/shard_map/all_to_all | solution.py:79
  89.2 1.1 fusion.41
  90.4 5.9 %custom-call.24 = f32[2,32,32]{2,1,0:T(8,128)S(1)} custom-call(f32[2,32,32]{2,1,0:T(8,128)S(1)} %fusion.24), custom_call_target="Cholesky" | custom-call | tf_op jit(solution)/shard_map/jit(cholesky)/cholesky | solution.py:28
  96.5 4.9 %custom-call.25 = f32[2,1,32,32]{2,3,1,0:T(8,128)S(1)} custom-call(f32[2,1,32,32]{3,2,1,0:T(8,128)S(1)} %select_bitcast_fusion.2), custom_call_target="InvertDiagBlocksLowerTriangular" | custom-call | tf_op jit(solution)/shard_map/jit(_solve_triangular)/vmap()/triangular_solve | solution.py:29
  102.5 2.7 %fusion.8 = f32[2,32,4096]{2,1,0:T(8,128)S(1)} fusion(bf16[2,32,4096]{2,1,0:T(8,128)(2,1)S(1)} %convolution_convert_fusion.2, bf16[1,4096,128]{2,1,0:T(8,128)(2,1)} %bitcast.165, bf16[1,4096,128]{2,1,0:T(8,128)(2,1)S(1)} %bitcast.161), kind=kOutput, calls=%fused_computation.29 | convolution fusion | flops 136323072 | bytes 3670016 | tf_op jit(solution)/shard_map/prf,pkf->prk/dot_general | solution.py:19
  106.4 5.9 %custom-call.26 = f32[2,32,32]{2,1,0:T(8,128)S(1)} custom-call(f32[2,32,32]{2,1,0:T(8,128)S(1)} %fusion.22), custom_call_target="Cholesky" | custom-call | tf_op jit(solution)/shard_map/jit(cholesky)/cholesky | solution.py:28
  112.5 4.9 %custom-call.27 = f32[2,1,32,32]{2,3,1,0:T(8,128)S(1)} custom-call(f32[2,1,32,32]{3,2,1,0:T(8,128)S(1)} %select_bitcast_fusion.1), custom_call_target="InvertDiagBlocksLowerTriangular" | custom-call | tf_op jit(solution)/shard_map/jit(_solve_triangular)/vmap()/triangular_solve | solution.py:29
  118.5 2.7 %fusion.9 = f32[2,32,4096]{2,1,0:T(8,128)S(1)} fusion(bf16[2,32,4096]{2,1,0:T(8,128)(2,1)S(1)} %convolution_convert_fusion.1, bf16[1,4096,128]{2,1,0:T(8,128)(2,1)} %bitcast.166, bf16[1,4096,128]{2,1,0:T(8,128)(2,1)S(1)} %bitcast.162), kind=kOutput, calls=%fused_computation.30 | convolution fusion | flops 136323072 | bytes 3670016 | tf_op jit(solution)/shard_map/prf,pkf->prk/dot_general | solution.py:19
  122.4 5.9 %custom-call.28 = f32[2,32,32]{2,1,0:T(8,128)S(1)} custom-call(f32[2,32,32]{2,1,0:T(8,128)S(1)} %fusion.20), custom_call_target="Cholesky" | custom-call | tf_op jit(solution)/shard_map/jit(cholesky)/cholesky | solution.py:28
  128.5 5.1 %custom-call.29 = f32[2,1,32,32]{2,3,1,0:T(8,128)S(1)} custom-call(f32[2,1,32,32]{3,2,1,0:T(8,128)S(1)} %select_bitcast_fusion), custom_call_target="InvertDiagBlocksLowerTriangular" | custom-call | tf_op jit(solution)/shard_map/jit(_solve_triangular)/vmap()/triangular_solve | solution.py:29
  134.8 1.7 fusion
  136.7 1.8 %fusion.1 = bf16[8,32,2,32]{1,0,3,2:T(8,128)(2,1)S(1)} fusion(f32[8,32,2,8]{1,3,0,2:T(8,128)S(1)} %copy-done.4, bf16[2,32,16,256]{3,2,1,0:T(8,128)(2,1)S(1)} %bitcast.170, bf16[8,32,2,256]{3,1,2,0:T(8,128)(2,1)} %all-to-all-done.1), kind=kOutput, calls=%fused_computation.17 | convolution fusion | flops 67354624 | bytes 491520 | tf_op jit(solution)/shard_map/nkb,prgb->nkpgr/dot_general | solution.py:85
  139.5 5.1 %all-to-all-start.2 = ((bf16[8,2,2048]{2,1,0:T(2,128)(2,1)}), bf16[8,2,2048]{2,1,0:T(2,128)(2,1)S(1)}, u32[]{:S(2)}, u32[]{:S(2)}) async-start(bf16[8,2,2048]{2,1,0:T(2,128)(2,1)} %reshape.613), calls=%async_computation.2 | async-start | bytes 131072 | tf_op jit(solution)/shard_map/all_to_all | solution.py:105
  144.6 1.1 fusion.40
  145.7 14.5 %all_gather.3 = bf16[16,32,128]{2,1,0:T(8,128)(2,1)S(1)} all-gather(bf16[2,32,128]{2,1,0:T(8,128)(2,1)S(1)} %get-tuple-element.26), channel_id=1, replica_groups=mesh['plane'=4,'tile'=8] {'tile'}, dimensions={0}, use_global_device_ids=true | all-gather | bytes 147456 | tf_op jit(solution)/shard_map/all_gather | solution.py:112
  163.0 10.6 %gather_fusion.2 = bf16[2048,32]{1,0:T(8,128)(2,1)S(1)} fusion(bf16[128,5,32]{2,0,1:T(8,128)(2,1)S(1)} %copy.61, s32[2048]{0:T(1024)S(1)} %reshape.577), kind=kCustom, calls=%fused_computation.2 | custom fusion | bytes 278528 | tf_op jit(solution)/shard_map/jit(take_along_axis)/gather | solution.py:126
  (94 shorter events, 16.7 us)
Async XLA Ops:
  0.6 43.7 %copy-start = (bf16[1,1,3,4,256,128]{5,4,3,2,1,0:T(8,128)(2,1)S(1)}, bf16[1,1,3,4,256,128]{5,4,3,2,1,0:T(8,128)(2,1)}, u32[]{:S(2)}) copy-start(bf16[1,1,3,4,256,128]{5,4,3,2,1,0:T(8,128)(2,1)} %param.8) | copy-start | bytes 2359300
  0.6 45.2 %copy-start.5 = (s32[1,128,1]{1,2,0:T(1,128)S(1)}, s32[1,128,1]{1,2,0:T(1,128)}, u32[]{:S(2)}) copy-start(s32[1,128,1]{1,2,0:T(1,128)} %param.11) | copy-start | bytes 1540
  2.3 44.0 %copy-start.6 = (s32[1,128]{1,0:T(1,128)S(1)}, s32[1,128]{1,0:T(1,128)}, u32[]{:S(2)}) copy-start(s32[1,128]{1,0:T(1,128)} %param.12) | copy-start | bytes 1540
  44.5 43.1 %collective-permute-start = (bf16[3,4,256,128]{3,2,1,0:T(8,128)(2,1)S(1)}, bf16[3,4,256,128]{3,2,1,0:T(8,128)(2,1)S(1)}, u32[]{:S(2)}, u32[]{:S(2)}) collective-permute-start(bf16[3,4,256,128]{3,2,1,0:T(8,128)(2,1)S(1)} %fusion.5), channel_id=1, source_target_pairs={{2,0},{3,1},{4,2},{5,3},{6,4},{7,5},{10,8},{11,9},{12,10},{13,11},... | collective-permute-start | bytes 2359304 | tf_op jit(solution)/shard_map/ppermute | solution.py:12
  60.0 7.0 %copy-start.3 = (bf16[1,128,256]{2,1,0:T(8,128)(2,1)S(1)}, bf16[1,128,256]{2,1,0:T(8,128)(2,1)}, u32[]{:S(2)}) copy-start(bf16[1,128,256]{2,1,0:T(8,128)(2,1)} %param.10) | copy-start | bytes 196612
  60.7 20.9 %all-to-all-start = ((s32[8,32,2]{1,2,0:T(2,128)}), s32[8,32,2]{1,2,0:T(2,128)S(1)}, u32[]{:S(2)}, u32[]{:S(2)}) async-start(s32[8,32,2]{1,2,0:T(2,128)} %copy.50), calls=%async_computation | async-start | bytes 16384 | tf_op jit(solution)/shard_map/all_to_all | solution.py:80
  81.6 53.1 %all-to-all-start.1 = ((bf16[8,32,2,256]{3,1,2,0:T(8,128)(2,1)}), bf16[8,32,2,256]{3,1,2,0:T(8,128)(2,1)}, u32[]{:S(2)}, u32[]{:S(2)}) async-start(bf16[8,32,2,256]{3,1,2,0:T(8,128)(2,1)} %copy.52), calls=%async_computation.1 | async-start | bytes 524288 | tf_op jit(solution)/shard_map/all_to_all | solution.py:79
  87.6 0.8 copy-start.7
  87.8 1.4 copy-start.1
  134.8 1.9 %copy-start.4 = (f32[8,32,2,8]{1,3,0,2:T(8,128)S(1)}, f32[8,32,2,8]{1,3,0,2:T(8,128)}, u32[]{:S(2)}) copy-start(f32[8,32,2,8]{1,3,0,2:T(8,128)} %and_convert_fusion.1) | copy-start | bytes 49156
  136.7 7.9 %copy-start.2 = (bf16[2,2,4,256,128]{4,3,2,1,0:T(8,128)(2,1)S(1)}, bf16[2,2,4,256,128]{4,3,2,1,0:T(8,128)(2,1)}, u32[]{:S(2)}) copy-start(bf16[2,2,4,256,128]{4,3,2,1,0:T(8,128)(2,1)} %copy-done.1) | copy-start | bytes 3145732
  139.5 20.7 %all-to-all-start.2 = ((bf16[8,2,2048]{2,1,0:T(2,128)(2,1)}), bf16[8,2,2048]{2,1,0:T(2,128)(2,1)S(1)}, u32[]{:S(2)}, u32[]{:S(2)}) async-start(bf16[8,2,2048]{2,1,0:T(2,128)(2,1)} %reshape.613), calls=%async_computation.2 | async-start | bytes 131072 | tf_op jit(solution)/shard_map/all_to_all | solution.py:105
where the time goes:
time: 175 us
  blocking collectives  56.5 us (32%)
  local copies, waits for them, and re-layouts  44.8 us (26%)
  other arithmetic  37 us (21%)
  matrix products  18.2 us (10%)
  starting transfers between devices  17.2 us (10%)
    psum x1, blocking collectives, on_device(): background = lax.psum(frame_sum, ('plane', 'tile')) / pixel_total  42 us
    another operation x10, other arithmetic, compress_patches(): cholesky_factor = jnp.linalg.cholesky(gram_matrix)  18.1 us
    another operation x7, other arithmetic, compress_patches(): jax.scipy.linalg.solve_triangular(cholesky_factor, projection, lower=True)  15.2 us
    all_gather x1, blocking collectives, on_device(): shard_rows = lax.all_gather(temporal_rounded, 'tile', axis=0, tiled=True)  14.5 us
    scatter x2, local copies, waits for them, and re-layouts, on_device(): block_send.at[slot_upper, 0].set(block_value).at[slot_lower, 1]  13.7 us
    scatter x2, local copies, waits for them, and re-layouts, on_device(): footprint_send.at[slot_upper, 0].set(footprint_rows).at[slot_lower, 1]  13.6 us
    gather x3, local copies, waits for them, and re-layouts, on_device(): weights = jnp.take_along_axis(coef_table, lookup[:, :, None], axis=1)  11.1 us
    dot_general x3, matrix products, compress_patches(): jnp.einsum('prf,pkf->prk', temporal.astype(jnp.bfloat16), patches, prefer...  6.26 us
  transfers between devices with their start and end apart: 4, of which 0 were waited for; matrix products, arithmetic and copies ran while one was open for 45% of the time, Pallas kernels for 0%

commit v1 on v0

--- a/solution.py
+++ b/solution.py
@@ -102,7 +102,21 @@
             )
         )
     coefficient = jnp.stack(role_terms, 2).astype(jnp.bfloat16)
-    replies = lax.all_to_all(coefficient, "tile", split_axis=0, concat_axis=0, tiled=True)
+    vec_out, oldest = (lax.psum(1, axis_name="tile"), lax.axis_index("tile"))
+    earlier = coefficient.shape[0] // vec_out
+    x_new = list(coefficient.shape)
+    x_new[0] = earlier
+    upper = x_new[0]
+    x_new[0] = upper * vec_out
+    replies = jnp.zeros(x_new, coefficient.dtype)
+    for d in tuple(range(vec_out)):
+        near = lax.dynamic_slice_in_dim(coefficient, (oldest ^ d) * earlier, earlier, axis=0)
+        if d:
+            in_order = []
+            for idx in [*range(vec_out)]:
+                in_order.append((idx, idx ^ d))
+            near = lax.ppermute(near, axis_name="tile", perm=in_order)
+        replies = lax.dynamic_update_slice_in_dim(replies, near, (oldest ^ d) * upper, axis=0)
     reply_rows = replies.reshape(tile_count * capacity, 2, patch_count * rank_width)
     upper_coefs = reply_rows[slot_upper, 0].reshape(source_count, patch_count, rank_width)
     lower_coefs = reply_rows[slot_lower, 1].reshape(source_count, patch_count, rank_width)

time: 175 us -> 183 us (1.046)
  waiting for transfers between devices: 0.01 us -> 4.88 us
  starting transfers between devices: 17.2 us -> 20.4 us
    ppermute x0 -> x7, starting transfers between devices: none -> 8.31 us  [on_device(): near = lax.ppermute(near, axis_name='tile', perm=in_order)]
    all_to_all x1 -> x0, starting transfers between devices: 5.1 us -> none  [on_device(): lax.all_to_all(coefficient, 'tile', split_axis=0, concat_axis=0, tiled=True)]
    ppermute x0 -> x7, waiting for transfers between devices: none -> 4.87 us  [on_device(): near = lax.ppermute(near, axis_name='tile', perm=in_order)]
  transfers between devices with their start and end apart: 4 -> 10, of which waited for: 0 -> 2; matrix products, arithmetic and copies ran while one was open for 45% -> 43% of each run, Pallas kernels for 0% -> 0%
where the time goes in v1:
time: 183 us; the launch traced here: 182 us
  blocking collectives  56.8 us (31%)
  local copies, waits for them, and re-layouts  44 us (24%)
  other arithmetic  36.8 us (20%)
  starting transfers between devices  20.4 us (11%)
  matrix products  18.2 us (10%)
  waiting for transfers between devices  4.88 us (3%)
    psum x1, blocking collectives, on_device(): background = lax.psum(frame_sum, ('plane', 'tile')) / pixel_total  42 us
    another operation x10, other arithmetic, compress_patches(): cholesky_factor = jnp.linalg.cholesky(gram_matrix)  18.1 us
    another operation x7, other arithmetic, compress_patches(): jax.scipy.linalg.solve_triangular(cholesky_factor, projection, lower=True)  15 us
    all_gather x1, blocking collectives, on_device(): shard_rows = lax.all_gather(temporal_rounded, 'tile', axis=0, tiled=True)  14.7 us
    scatter x2, local copies, waits for them, and re-layouts, on_device(): block_send.at[slot_upper, 0].set(block_value).at[slot_lower, 1]  13.7 us
    scatter x2, local copies, waits for them, and re-layouts, on_device(): footprint_send.at[slot_upper, 0].set(footprint_rows).at[slot_lower, 1]  13.6 us
    gather x3, local copies, waits for them, and re-layouts, on_device(): weights = jnp.take_along_axis(coef_table, lookup[:, :, None], axis=1)  11.1 us
    ppermute x7, starting transfers between devices, on_device(): near = lax.ppermute(near, axis_name='tile', perm=in_order)  8.31 us
  transfers between devices with their start and end apart: 10, of which 2 were waited for; matrix products, arithmetic and copies ran while one was open for 43% of the time, Pallas kernels for 0%

profile of v1, /device:TPU:0, one launch (start us, length us, event | category | flops | bytes accessed | tf_op | source)
XLA Modules:
  0.0 182.3 jit_solution(1928909996321195826)
XLA Ops:
  0.6 1.6 convert_reduce_fusion
  2.3 42.0 %psum.7 = f32[128]{0:T(128)S(1)} all-reduce(f32[128]{0:T(128)S(1)} %convert_reduce_fusion), channel_id=1, replica_groups=mesh['plane'=4,'tile'=8] {'plane','tile'}, use_global_device_ids=true, to_apply=%region_1.0 | all-reduce | flops 128 | bytes 1024 | tf_op jit(solution)/shard_map/psum | solution.py:45
  46.3 6.8 %scatter_fusion = s32[256,2]{0,1:T(2,128)S(1)} fusion(s32[256,2]{0,1:T(2,128)S(1)} %broadcast_in_dim.85, s32[128]{0:T(128)S(1)} %fusion.41, s32[128]{0:T(128)S(1)} %bitcast.182), kind=kCustom, calls=%fused_computation.3 | custom fusion | bytes 2560 | tf_op jit(solution)/shard_map/scatter | solution.py:73
  53.2 6.8 %scatter_fusion.1 = s32[256,2]{0,1:T(2,128)S(1)} fusion(s32[256,2]{0,1:T(2,128)S(1)} %scatter_fusion, s32[128]{0:T(128)S(1)} %fusion.42, s32[128]{0:T(128)S(1)} %bitcast.183), kind=kCustom, calls=%fused_computation.4 | custom fusion | bytes 2560 | tf_op jit(solution)/shard_map/scatter | solution.py:73
  60.8 5.7 %all-to-all-start = ((s32[8,32,2]{1,2,0:T(2,128)}), s32[8,32,2]{1,2,0:T(2,128)S(1)}, u32[]{:S(2)}, u32[]{:S(2)}) async-start(s32[8,32,2]{1,2,0:T(2,128)} %copy.63), calls=%async_computation | async-start | bytes 16384 | tf_op jit(solution)/shard_map/all_to_all | solution.py:80
  67.1 6.8 %scatter_fusion.2 = bf16[256,2,256]{2,1,0:T(2,128)(2,1)S(1)} fusion(bf16[256,2,256]{2,1,0:T(2,128)(2,1)S(1)} %broadcast_in_dim.86, s32[128]{0:T(128)S(1)} %fusion.41, bf16[128,256]{1,0:T(8,128)(2,1)S(1)} %bitcast.168), kind=kCustom, calls=%fused_computation.5 | custom fusion | bytes 197632 | tf_op jit(solution)/shard_map/scatter | solution.py:70
  74.0 6.8 %scatter_fusion.3 = bf16[256,2,256]{2,1,0:T(2,128)(2,1)S(1)} fusion(bf16[256,2,256]{2,1,0:T(2,128)(2,1)S(1)} %scatter_fusion.2, s32[128]{0:T(128)S(1)} %fusion.42, bf16[128,256]{1,0:T(8,128)(2,1)S(1)} %bitcast.169), kind=kCustom, calls=%fused_computation.6 | custom fusion | bytes 197632 | tf_op jit(solution)/shard_map/scatter | solution.py:70
  81.7 5.1 %all-to-all-start.1 = ((bf16[8,32,2,256]{3,1,2,0:T(8,128)(2,1)}), bf16[8,32,2,256]{3,1,2,0:T(8,128)(2,1)}, u32[]{:S(2)}, u32[]{:S(2)}) async-start(bf16[8,32,2,256]{3,1,2,0:T(8,128)(2,1)} %copy.65), calls=%async_computation.1 | async-start | bytes 524288 | tf_op jit(solution)/shard_map/all_to_all | solution.py:79
  90.4 5.9 %custom-call.24 = f32[2,32,32]{2,1,0:T(8,128)S(1)} custom-call(f32[2,32,32]{2,1,0:T(8,128)S(1)} %fusion.24), custom_call_target="Cholesky" | custom-call | tf_op jit(solution)/shard_map/jit(cholesky)/cholesky | solution.py:28
  96.5 4.9 %custom-call.25 = f32[2,1,32,32]{2,3,1,0:T(8,128)S(1)} custom-call(f32[2,1,32,32]{3,2,1,0:T(8,128)S(1)} %select_bitcast_fusion.2), custom_call_target="InvertDiagBlocksLowerTriangular" | custom-call | tf_op jit(solution)/shard_map/jit(_solve_triangular)/vmap()/triangular_solve | solution.py:29
  102.5 2.7 %fusion.8 = f32[2,32,4096]{2,1,0:T(8,128)S(1)} fusion(bf16[2,32,4096]{2,1,0:T(8,128)(2,1)S(1)} %convolution_convert_fusion.2, bf16[1,4096,128]{2,1,0:T(8,128)(2,1)} %bitcast.162, bf16[1,4096,128]{2,1,0:T(8,128)(2,1)S(1)} %bitcast.158), kind=kOutput, calls=%fused_computation.29 | convolution fusion | flops 136323072 | bytes 3670016 | tf_op jit(solution)/shard_map/prf,pkf->prk/dot_general | solution.py:19
  106.4 5.9 %custom-call.26 = f32[2,32,32]{2,1,0:T(8,128)S(1)} custom-call(f32[2,32,32]{2,1,0:T(8,128)S(1)} %fusion.22), custom_call_target="Cholesky" | custom-call | tf_op jit(solution)/shard_map/jit(cholesky)/cholesky | solution.py:28
  112.5 4.9 %custom-call.27 = f32[2,1,32,32]{2,3,1,0:T(8,128)S(1)} custom-call(f32[2,1,32,32]{3,2,1,0:T(8,128)S(1)} %select_bitcast_fusion.1), custom_call_target="InvertDiagBlocksLowerTriangular" | custom-call | tf_op jit(solution)/shard_map/jit(_solve_triangular)/vmap()/triangular_solve | solution.py:29
  118.5 2.7 %fusion.9 = f32[2,32,4096]{2,1,0:T(8,128)S(1)} fusion(bf16[2,32,4096]{2,1,0:T(8,128)(2,1)S(1)} %convolution_convert_fusion.1, bf16[1,4096,128]{2,1,0:T(8,128)(2,1)} %bitcast.163, bf16[1,4096,128]{2,1,0:T(8,128)(2,1)S(1)} %bitcast.159), kind=kOutput, calls=%fused_computation.30 | convolution fusion | flops 136323072 | bytes 3670016 | tf_op jit(solution)/shard_map/prf,pkf->prk/dot_general | solution.py:19
  122.4 5.9 %custom-call.28 = f32[2,32,32]{2,1,0:T(8,128)S(1)} custom-call(f32[2,32,32]{2,1,0:T(8,128)S(1)} %fusion.20), custom_call_target="Cholesky" | custom-call | tf_op jit(solution)/shard_map/jit(cholesky)/cholesky | solution.py:28
  128.5 4.9 %custom-call.29 = f32[2,1,32,32]{2,3,1,0:T(8,128)S(1)} custom-call(f32[2,1,32,32]{3,2,1,0:T(8,128)S(1)} %select_bitcast_fusion), custom_call_target="InvertDiagBlocksLowerTriangular" | custom-call | tf_op jit(solution)/shard_map/jit(_solve_triangular)/vmap()/triangular_solve | solution.py:29
  135.8 14.7 %all_gather.3 = bf16[16,32,128]{2,1,0:T(8,128)(2,1)S(1)} all-gather(bf16[2,32,128]{2,1,0:T(8,128)(2,1)S(1)} %get-tuple-element.34), channel_id=1, replica_groups=mesh['plane'=4,'tile'=8] {'tile'}, dimensions={0}, use_global_device_ids=true | all-gather | bytes 147456 | tf_op jit(solution)/shard_map/all_gather | solution.py:126
  150.5 1.8 fusion.1
  152.4 1.7 fusion
  156.3 2.3 %collective-permute-start.4 = (bf16[1,32,2,64]{3,1,0,2:T(8,128)(2,1)S(1)}, bf16[1,32,2,64]{3,1,0,2:T(8,128)(2,1)S(1)}, u32[]{:S(2)}, u32[]{:S(2)}) collective-permute-start(bf16[1,32,2,64]{3,1,0,2:T(8,128)(2,1)S(1)} %get-tuple-element.19), channel_id=1, source_target_pairs={{0,4},{1,5},{2,6},{3,7},{4,0},{5,1},{6,2},{7,3},{8,12},{9,13},{10,... | collective-permute-start | bytes 24584 | tf_op jit(solution)/shard_map/ppermute | solution.py:118
  159.3 3.3 %collective-permute-start.6 = (bf16[1,32,2,64]{3,1,0,2:T(8,128)(2,1)S(1)}, bf16[1,32,2,64]{3,1,0,2:T(8,128)(2,1)S(1)}, u32[]{:S(2)}, u32[]{:S(2)}) collective-permute-start(bf16[1,32,2,64]{3,1,0,2:T(8,128)(2,1)S(1)} %get-tuple-element.20), channel_id=1, source_target_pairs={{0,6},{1,7},{2,4},{3,5},{4,2},{5,3},{6,0},{7,1},{8,14},{9,15},{10,... | collective-permute-start | bytes 24584 | tf_op jit(solution)/shard_map/ppermute | solution.py:118
  163.0 2.0 %collective-permute-done.6 = bf16[1,32,2,64]{3,1,0,2:T(8,128)(2,1)S(1)} collective-permute-done((bf16[1,32,2,64]{3,1,0,2:T(8,128)(2,1)S(1)}, bf16[1,32,2,64]{3,1,0,2:T(8,128)(2,1)S(1)}, u32[]{:S(2)}, u32[]{:S(2)}) %collective-permute-start.6) | collective-permute-done | bytes 8224 | tf_op jit(solution)/shard_map/ppermute | solution.py:118
  165.0 2.9 %collective-permute-done.7 = bf16[1,32,2,64]{3,1,0,2:T(8,128)(2,1)S(1)} collective-permute-done((bf16[1,32,2,64]{3,1,0,2:T(8,128)(2,1)S(1)}, bf16[1,32,2,64]{3,1,0,2:T(8,128)(2,1)S(1)}, u32[]{:S(2)}, u32[]{:S(2)}) %collective-permute-start.7) | collective-permute-done | bytes 8224 | tf_op jit(solution)/shard_map/ppermute | solution.py:118
  170.4 10.6 %gather_fusion.2 = bf16[2048,32]{1,0:T(8,128)(2,1)S(1)} fusion(bf16[128,5,32]{2,0,1:T(8,128)(2,1)S(1)} %copy.80, s32[2048]{0:T(1024)S(1)} %reshape.577), kind=kCustom, calls=%fused_computation.2 | custom fusion | bytes 278528 | tf_op jit(solution)/shard_map/jit(take_along_axis)/gather | solution.py:140
  (112 shorter events, 22.2 us)
Async XLA Ops:
  0.6 43.7 %copy-start = (bf16[1,1,3,4,256,128]{5,4,3,2,1,0:T(8,128)(2,1)S(1)}, bf16[1,1,3,4,256,128]{5,4,3,2,1,0:T(8,128)(2,1)}, u32[]{:S(2)}) copy-start(bf16[1,1,3,4,256,128]{5,4,3,2,1,0:T(8,128)(2,1)} %param.8) | copy-start | bytes 2359300
  0.6 45.2 %copy-start.5 = (s32[1,128,1]{1,2,0:T(1,128)S(1)}, s32[1,128,1]{1,2,0:T(1,128)}, u32[]{:S(2)}) copy-start(s32[1,128,1]{1,2,0:T(1,128)} %param.11) | copy-start | bytes 1540
  2.3 44.1 %copy-start.6 = (s32[1,128]{1,0:T(1,128)S(1)}, s32[1,128]{1,0:T(1,128)}, u32[]{:S(2)}) copy-start(s32[1,128]{1,0:T(1,128)} %param.12) | copy-start | bytes 1540
  44.5 43.1 %collective-permute-start = (bf16[3,4,256,128]{3,2,1,0:T(8,128)(2,1)S(1)}, bf16[3,4,256,128]{3,2,1,0:T(8,128)(2,1)S(1)}, u32[]{:S(2)}, u32[]{:S(2)}) collective-permute-start(bf16[3,4,256,128]{3,2,1,0:T(8,128)(2,1)S(1)} %fusion.5), channel_id=1, source_target_pairs={{2,0},{3,1},{4,2},{5,3},{6,4},{7,5},{10,8},{11,9},{12,10},{13,11},... | collective-permute-start | bytes 2359304 | tf_op jit(solution)/shard_map/ppermute | solution.py:12
  60.1 7.1 %copy-start.3 = (bf16[1,128,256]{2,1,0:T(8,128)(2,1)S(1)}, bf16[1,128,256]{2,1,0:T(8,128)(2,1)}, u32[]{:S(2)}) copy-start(bf16[1,128,256]{2,1,0:T(8,128)(2,1)} %param.10) | copy-start | bytes 196612
  60.8 20.9 %all-to-all-start = ((s32[8,32,2]{1,2,0:T(2,128)}), s32[8,32,2]{1,2,0:T(2,128)S(1)}, u32[]{:S(2)}, u32[]{:S(2)}) async-start(s32[8,32,2]{1,2,0:T(2,128)} %copy.63), calls=%async_computation | async-start | bytes 16384 | tf_op jit(solution)/shard_map/all_to_all | solution.py:80
  81.7 68.8 %all-to-all-start.1 = ((bf16[8,32,2,256]{3,1,2,0:T(8,128)(2,1)}), bf16[8,32,2,256]{3,1,2,0:T(8,128)(2,1)}, u32[]{:S(2)}, u32[]{:S(2)}) async-start(bf16[8,32,2,256]{3,1,2,0:T(8,128)(2,1)} %copy.65), calls=%async_computation.1 | async-start | bytes 524288 | tf_op jit(solution)/shard_map/all_to_all | solution.py:79
  87.7 0.8 copy-start.7
  87.8 1.4 copy-start.1
  133.4 1.3 copy-start.2
  150.5 1.9 %copy-start.4 = (f32[8,32,2,8]{1,3,0,2:T(8,128)S(1)}, f32[8,32,2,8]{1,3,0,2:T(8,128)}, u32[]{:S(2)}) copy-start(f32[8,32,2,8]{1,3,0,2:T(8,128)} %and_convert_fusion) | copy-start | bytes 49156
  154.3 5.0 %collective-permute-start.1 = (bf16[1,32,2,64]{3,1,0,2:T(8,128)(2,1)S(1)}, bf16[1,32,2,64]{3,1,0,2:T(8,128)(2,1)S(1)}, u32[]{:S(2)}, u32[]{:S(2)}) collective-permute-start(bf16[1,32,2,64]{3,1,0,2:T(8,128)(2,1)S(1)} %get-tuple-element.16), channel_id=1, source_target_pairs={{0,1},{1,0},{2,3},{3,2},{4,5},{5,4},{6,7},{7,6},{8,9},{9,8},{10,11... | collective-permute-start | bytes 24584 | tf_op jit(solution)/shard_map/ppermute | solution.py:118
  154.7 8.0 %collective-permute-start.2 = (bf16[1,32,2,64]{3,1,0,2:T(8,128)(2,1)S(1)}, bf16[1,32,2,64]{3,1,0,2:T(8,128)(2,1)S(1)}, u32[]{:S(2)}, u32[]{:S(2)}) collective-permute-start(bf16[1,32,2,64]{3,1,0,2:T(8,128)(2,1)S(1)} %get-tuple-element.17), channel_id=1, source_target_pairs={{0,2},{1,3},{2,0},{3,1},{4,6},{5,7},{6,4},{7,5},{8,10},{9,11},{10,... | collective-permute-start | bytes 24584 | tf_op jit(solution)/shard_map/ppermute | solution.py:118
  156.2 6.6 %collective-permute-start.3 = (bf16[1,32,2,64]{3,1,0,2:T(8,128)(2,1)S(1)}, bf16[1,32,2,64]{3,1,0,2:T(8,128)(2,1)S(1)}, u32[]{:S(2)}, u32[]{:S(2)}) collective-permute-start(bf16[1,32,2,64]{3,1,0,2:T(8,128)(2,1)S(1)} %get-tuple-element.18), channel_id=1, source_target_pairs={{0,3},{1,2},{2,1},{3,0},{4,7},{5,6},{6,5},{7,4},{8,11},{9,10},{10,... | collective-permute-start | bytes 24584 | tf_op jit(solution)/shard_map/ppermute | solution.py:118
  156.3 6.6 %collective-permute-start.4 = (bf16[1,32,2,64]{3,1,0,2:T(8,128)(2,1)S(1)}, bf16[1,32,2,64]{3,1,0,2:T(8,128)(2,1)S(1)}, u32[]{:S(2)}, u32[]{:S(2)}) collective-permute-start(bf16[1,32,2,64]{3,1,0,2:T(8,128)(2,1)S(1)} %get-tuple-element.19), channel_id=1, source_target_pairs={{0,4},{1,5},{2,6},{3,7},{4,0},{5,1},{6,2},{7,3},{8,12},{9,13},{10,... | collective-permute-start | bytes 24584 | tf_op jit(solution)/shard_map/ppermute | solution.py:118
  158.6 4.3 %collective-permute-start.5 = (bf16[1,32,2,64]{3,1,0,2:T(8,128)(2,1)S(1)}, bf16[1,32,2,64]{3,1,0,2:T(8,128)(2,1)S(1)}, u32[]{:S(2)}, u32[]{:S(2)}) collective-permute-start(bf16[1,32,2,64]{3,1,0,2:T(8,128)(2,1)S(1)} %get-tuple-element.21), channel_id=1, source_target_pairs={{0,5},{1,4},{2,7},{3,6},{4,1},{5,0},{6,3},{7,2},{8,13},{9,12},{10,... | collective-permute-start | bytes 24584 | tf_op jit(solution)/shard_map/ppermute | solution.py:118
  159.3 5.6 %collective-permute-start.6 = (bf16[1,32,2,64]{3,1,0,2:T(8,128)(2,1)S(1)}, bf16[1,32,2,64]{3,1,0,2:T(8,128)(2,1)S(1)}, u32[]{:S(2)}, u32[]{:S(2)}) collective-permute-start(bf16[1,32,2,64]{3,1,0,2:T(8,128)(2,1)S(1)} %get-tuple-element.20), channel_id=1, source_target_pairs={{0,6},{1,7},{2,4},{3,5},{4,2},{5,3},{6,0},{7,1},{8,14},{9,15},{10,... | collective-permute-start | bytes 24584 | tf_op jit(solution)/shard_map/ppermute | solution.py:118
  162.7 5.1 %collective-permute-start.7 = (bf16[1,32,2,64]{3,1,0,2:T(8,128)(2,1)S(1)}, bf16[1,32,2,64]{3,1,0,2:T(8,128)(2,1)S(1)}, u32[]{:S(2)}, u32[]{:S(2)}) collective-permute-start(bf16[1,32,2,64]{3,1,0,2:T(8,128)(2,1)S(1)} %get-tuple-element.14), channel_id=1, source_target_pairs={{0,7},{1,6},{2,5},{3,4},{4,3},{5,2},{6,1},{7,0},{8,15},{9,14},{10,... | collective-permute-start | bytes 24584 | tf_op jit(solution)/shard_map/ppermute | solution.py:118
